TPU v7x, 32 devices: a whole 2x2x4 slice. The times are simulated.
32 devices in a mesh: dp: 8 (over z, core), seq: 4 (over y, x).
Axes of the slice: x: 2, y: 2, z: 4, core: 2. Of those that a mesh axis runs over, the one named last changes fastest.
Arguments:
- tokens: bfloat16 [1024, 4096], P(('dp', 'seq')), may hold values from -6 to 6
- modality: int32 [1024], P(('dp', 'seq')), may hold values from 0 to 1, as said below
- gate_weight: bfloat16 [4096, 14336], P(None, 'dp'), may hold values from -0.09375 to 0.09375
- up_weight: bfloat16 [4096, 14336], P(None, 'dp'), may hold values from -0.09375 to 0.09375
- down_weight: bfloat16 [14336, 4096], P('dp'), may hold values from -0.046875 to 0.046875
- out_grad: bfloat16 [768, 4096], P(('dp', 'seq')), may hold values from -1.5 to 1.5
Outputs:
- output: bfloat16 [768, 4096], P(('dp', 'seq'))
- in_grad: bfloat16 [768, 4096], P(('dp', 'seq'))
- gate_grad: bfloat16 [4096, 14336], P('seq', 'dp')
- up_grad: bfloat16 [4096, 14336], P('seq', 'dp')
- down_grad: bfloat16 [14336, 4096], P('dp', 'seq')
Inputs may be any that keep to these rules, and one draw needn't show every extreme that they name: In each aligned block of 32 tokens (the tokens of one device) exactly 24 tokens have modality 1 (vision); all others have 0 (text).
All inputs are finite; a program needn't handle non-finite values.
Results may differ from a plain program's by a relative error of at most 0.014.
Values may be sent and summed in bfloat16 or wider, within the bound.
No kernel may reach another device: no remote copies, remote signals or barrier semaphores. Data moves between devices by JAX's collectives and lax.ppermute only.
A program may use at most 192 MiB of HBM per device.

v0:
```python
import jax
import jax.numpy as jnp
from jax import lax
from jax.sharding import PartitionSpec as P


def silu_parts(gate_proj):
    sigmoid_value = jax.nn.sigmoid(gate_proj)
    return (gate_proj * sigmoid_value, sigmoid_value * (1.0 + gate_proj * (1.0 - sigmoid_value)))


def contract_cols(left_matrix, right_matrix):
    return lax.dot_general(
        left_matrix, right_matrix, (((1,), (1,)), ((), ())), preferred_element_type=jnp.float32
    )


def group_sum(left_blocks, right_blocks, form):
    partials = jnp.einsum(
        form, left_blocks, right_blocks, preferred_element_type=jnp.float32
    ).astype(jnp.bfloat16)
    partials = lax.optimization_barrier(partials)
    return jnp.sum(partials.astype(jnp.float32), axis=0)


def on_device(tokens, modality, gate_weight, up_weight, down_weight, out_grad):
    vision_count = out_grad.shape[0]
    flags = (modality == 1).astype(jnp.int32)
    ranks = jnp.cumsum(flags) - 1
    slot_ids = jnp.arange(vision_count, dtype=jnp.int32)[:, None]
    selector = ((ranks[None, :] == slot_ids) & (flags[None, :] == 1)).astype(jnp.bfloat16)
    picked = jnp.dot(selector, tokens, preferred_element_type=jnp.float32).astype(jnp.bfloat16)
    token_rows = lax.all_gather(picked, "dp", axis=0, tiled=True)
    gate_proj = jnp.dot(token_rows, gate_weight, preferred_element_type=jnp.float32)
    up_proj = jnp.dot(token_rows, up_weight, preferred_element_type=jnp.float32)
    active, slope = silu_parts(gate_proj)
    hidden = (active * up_proj).astype(jnp.bfloat16)
    output = lax.psum_scatter(
        jnp.dot(hidden, down_weight, preferred_element_type=jnp.float32).astype(jnp.bfloat16),
        "dp",
        scatter_dimension=0,
        tiled=True,
    )
    cotangent_rows = lax.all_gather(out_grad, "dp", axis=0, tiled=True)
    back_hidden = contract_cols(cotangent_rows, down_weight)
    gate_back = (back_hidden * up_proj * slope).astype(jnp.bfloat16)
    up_back = (back_hidden * active).astype(jnp.bfloat16)
    in_grad = lax.psum_scatter(
        (contract_cols(gate_back, gate_weight) + contract_cols(up_back, up_weight)).astype(
            jnp.bfloat16
        ),
        "dp",
        scatter_dimension=0,
        tiled=True,
    )
    group_count = lax.axis_size("seq")
    row_total = token_rows.shape[0]
    split_tokens, split_cotangent = (
        lax.all_to_all(token_rows, "seq", split_axis=1, concat_axis=0, tiled=True),
        lax.all_to_all(cotangent_rows, "seq", split_axis=1, concat_axis=0, tiled=True),
    )
    all_hidden, all_gate_back, all_up_back = (
        lax.all_gather(hidden, "seq", axis=0, tiled=True),
        lax.all_gather(gate_back, "seq", axis=0, tiled=True),
        lax.all_gather(up_back, "seq", axis=0, tiled=True),
    )

    def per_group(matrix):
        return matrix.reshape(group_count, row_total, matrix.shape[1])

    gate_total = group_sum(per_group(split_tokens), per_group(all_gate_back), "jrd,jrf->jdf")
    up_total = group_sum(per_group(split_tokens), per_group(all_up_back), "jrd,jrf->jdf")
    down_total = group_sum(per_group(all_hidden), per_group(split_cotangent), "jrf,jrd->jfd")
    return (
        output,
        in_grad,
        gate_total.astype(jnp.bfloat16),
        up_total.astype(jnp.bfloat16),
        down_total.astype(jnp.bfloat16),
    )


def solution(mesh):
    placed = (
        P(("dp", "seq"), None),
        P(("dp", "seq")),
        P(None, "dp"),
        P(None, "dp"),
        P("dp", None),
        P(("dp", "seq"), None),
    )
    return jax.shard_map(
        on_device,
        mesh=mesh,
        in_specs=placed,
        out_specs=(
            P(("dp", "seq"), None),
            P(("dp", "seq"), None),
            P("seq", "dp"),
            P("seq", "dp"),
            P("dp", "seq"),
        ),
        check_vma=False,
    )
```

profile of v0, /device:TPU:0, one launch (start us, length us, event | category | flops | bytes accessed | tf_op | source)
XLA Modules:
  0.0 296.2 jit_solution(6966429705825907858)
XLA Ops:
  7.2 0.0 copy-start
  7.2 0.0 all-gather.6.cloned.1.call-start
  7.2 0.7 fusion.9
  7.9 0.1 copy.13
  8.0 0.1 reduce-window.8
  8.1 0.1 add_reduce_fusion
  8.2 0.0 copy-done
  8.2 0.9 convolution_convert_fusion.4
  9.1 0.0 all-gather.6.cloned.1.call-update
  9.1 0.0 all-gather.8.cloned.1.call-start
  9.1 0.7 all-gather.8.cloned.1.call-update
  9.8 0.0 all-gather.14.cloned.1.call-start
  9.9 28.3 %all-gather.6.cloned.1.call-done = bf16[192,4096]{1,0:T(8,128)(2,1)} async-done(((bf16[24,4096]{1,0:T(8,128)(2,1)}), bf16[192,4096]{1,0:T(8,128)(2,1)}) %all-gather.6.cloned.1.call-update) | async-done | bytes 1572880 | tf_op jit(solution)/shard_map/all_gather | solution.py:33
  38.2 9.3 %fusion.12 = f32[192,1792]{1,0:T(8,128)S(1)} fusion(bf16[192,4096]{1,0:T(8,128)(2,1)} %all-gather.6.cloned.1.call-done, bf16[4096,1792]{1,0:T(8,128)(2,1)} %param.9), kind=kOutput, calls=%fused_computation.26 | convolution fusion | flops 2818572288 | bytes 17629184 | tf_op jit(solution)/shard_map/dot_general | solution.py:35
  47.5 1.3 copy-done.5
  48.8 4.2 %fusion.11 = f32[192,1792]{1,0:T(8,128)} fusion(bf16[192,4096]{1,0:T(8,128)(2,1)S(1)} %copy-done.2, bf16[4096,1792]{1,0:T(8,128)(2,1)S(1)} %copy-done.5), kind=kOutput, calls=%fused_computation.25 | convolution fusion | flops 2818572288 | bytes 17629184 | tf_op jit(solution)/shard_map/dot_general | solution.py:34
  53.0 11.3 %all-gather.8.cloned.1.call-done = bf16[192,4096]{1,0:T(8,128)(2,1)} async-done(((bf16[24,4096]{1,0:T(8,128)(2,1)}), bf16[192,4096]{1,0:T(8,128)(2,1)}) %all-gather.8.cloned.1.call-update) | async-done | bytes 1572880 | tf_op jit(solution)/shard_map/all_gather | solution.py:44
  64.3 12.5 %multiply_convert_fusion = (bf16[192,1792]{1,0:T(8,128)(2,1)}, bf16[192,1792]{1,0:T(8,128)(2,1)}, bf16[192,1792]{1,0:T(8,128)(2,1)}) fusion(f32[192,1792]{1,0:T(8,128)} %fusion.11, f32[192,1792]{1,0:T(8,128)S(1)} %fusion.12, bf16[192,4096]{1,0:T(8,128)(2,1)} %all-gather.8.cloned.1.call-done, bf16[1792,4096]{1,0:T(8,128)(2,1)} %param.10), kind=kOutput, calls=%fused_computation.12 | convolution fusion | flops 2823733248 | bytes 21069824 | tf_op jit(solution)/shard_map/dot_general | solution.py:13
  76.8 0.0 all-gather.14.cloned.1.call-update
  76.8 0.0 all-gather.12.cloned.1.call-start
  76.9 0.5 all-gather.12.cloned.1.call-update
  77.4 0.0 all-gather.10.cloned.1.call-start
  77.5 0.5 all-gather.10.cloned.1.call-update
  78.0 0.0 reduce-scatter.3.cloned.1.call-start
  78.1 9.9 %convolution_convert_fusion.3 = bf16[192,4096]{1,0:T(8,128)(2,1)} fusion(bf16[192,1792]{1,0:T(8,128)(2,1)} %get-tuple-element.7, bf16[1792,4096]{1,0:T(8,128)(2,1)} %param.10), kind=kOutput, calls=%fused_computation.5 | convolution fusion | flops 2819358720 | bytes 16941056 | tf_op jit(solution)/shard_map/dot_general | solution.py:39
  88.0 0.0 reduce-scatter.3.cloned.1.call-update
  88.0 1.3 copy.20
  89.3 3.7 %all-to-all-start.1 = ((bf16[192,4,1024]{2,0,1:T(8,128)(2,1)}), bf16[192,4,1024]{2,0,1:T(8,128)(2,1)S(1)}, u32[]{:S(2)}, u32[]{:S(2)}) async-start(bf16[192,4,1024]{2,0,1:T(8,128)(2,1)} %bitcast.35), calls=%async_computation.3 | async-start | bytes 3145728 | tf_op jit(solution)/shard_map/all_to_all | solution.py:60
  93.1 1.3 copy.21
  94.4 11.7 %fusion.13 = f32[192,4096]{1,0:T(8,128)} fusion(bf16[192,1792]{1,0:T(8,128)(2,1)S(1)} %copy-done.4, bf16[4096,1792]{1,0:T(8,128)(2,1)} %param.8), kind=kOutput, calls=%fused_computation.27 | convolution fusion | flops 2818572288 | bytes 18513920 | tf_op jit(solution)/shard_map/dot_general | solution.py:13
  106.1 18.2 %all-to-all-done.1 = bf16[192,4,1024]{2,0,1:T(8,128)(2,1)S(1)} async-done(((bf16[192,4,1024]{2,0,1:T(8,128)(2,1)}), bf16[192,4,1024]{2,0,1:T(8,128)(2,1)S(1)}, u32[]{:S(2)}, u32[]{:S(2)}) %all-to-all-start.1) | async-done | bytes 1572896 | tf_op jit(solution)/shard_map/all_to_all | solution.py:60
  124.3 3.6 %all-to-all-start = ((bf16[192,4,1024]{2,0,1:T(8,128)(2,1)}), bf16[192,4,1024]{2,0,1:T(8,128)(2,1)S(1)}, u32[]{:S(2)}, u32[]{:S(2)}) async-start(bf16[192,4,1024]{2,0,1:T(8,128)(2,1)} %bitcast.37), calls=%async_computation.2 | async-start | bytes 3145728 | tf_op jit(solution)/shard_map/all_to_all | solution.py:59
  127.8 0.0 reduce-scatter.5.cloned.1.call-start
  127.9 12.3 %fusion = bf16[192,4096]{1,0:T(8,128)(2,1)} fusion(f32[192,4096]{1,0:T(8,128)} %fusion.13, bf16[192,1792]{1,0:T(8,128)(2,1)} %get-tuple-element.5, bf16[4096,1792]{1,0:T(8,128)(2,1)} %param.9), kind=kOutput, calls=%fused_computation.4 | convolution fusion | flops 2820145152 | bytes 20086784 | tf_op jit(solution)/shard_map/dot_general | solution.py:13
  140.2 0.0 reduce-scatter.5.cloned.1.call-update
  140.2 0.0 all-gather.14.cloned.1.call-done
  140.3 9.5 %convolution_convert_fusion = bf16[4,1792,1024]{2,1,0:T(8,128)(2,1)} fusion(bf16[4,192,1792]{2,1,0:T(8,128)(2,1)} %bitcast.40, bf16[192,4,1024]{2,0,1:T(8,128)(2,1)S(1)} %all-to-all-done.1), kind=kOutput, calls=%fused_computation | convolution fusion | flops 2825912320 | bytes 19005440 | tf_op jit(solution)/shard_map/jrf,jrd->jfd/dot_general | solution.py:19
  149.8 0.0 all-to-all-done
  149.8 24.9 %all-gather.12.cloned.1.call-done = bf16[768,1792]{1,0:T(8,128)(2,1)} async-done(((bf16[192,1792]{1,0:T(8,128)(2,1)}), bf16[768,1792]{1,0:T(8,128)(2,1)}) %all-gather.12.cloned.1.call-update) | async-done | bytes 2752528 | tf_op jit(solution)/shard_map/all_gather | solution.py:65
  174.7 9.2 %convolution_convert_fusion.1 = bf16[4,1024,1792]{2,1,0:T(8,128)(2,1)} fusion(bf16[4,192,1792]{2,1,0:T(8,128)(2,1)} %bitcast.38, bf16[192,4,1024]{2,0,1:T(8,128)(2,1)S(1)} %all-to-all-done), kind=kOutput, calls=%fused_computation.1 | convolution fusion | flops 2825912320 | bytes 19005440 | tf_op jit(solution)/shard_map/jrd,jrf->jdf/dot_general | solution.py:19
  183.9 11.1 %reduce_sum.38 = bf16[1792,1024]{1,0:T(8,128)(2,1)} reduce(bf16[4,1792,1024]{2,1,0:T(8,128)(2,1)} %convolution_convert_fusion, bf16[]{:T(256)} %constant.15.clone.1), dimensions={0}, to_apply=%region_5.6 | reduce | flops 5505024 | bytes 18350082 | tf_op jit(solution)/shard_map/reduce_sum | solution.py:23
  195.1 10.9 %reduce_sum.37 = bf16[1024,1792]{1,0:T(8,128)(2,1)} reduce(bf16[4,1024,1792]{2,1,0:T(8,128)(2,1)} %convolution_convert_fusion.1, bf16[]{:T(256)} %constant.15.clone.1), dimensions={0}, to_apply=%region_4.5 | reduce | flops 5505024 | bytes 18350082 | tf_op jit(solution)/shard_map/reduce_sum | solution.py:23
  206.0 11.0 %all-gather.10.cloned.1.call-done = bf16[768,1792]{1,0:T(8,128)(2,1)} async-done(((bf16[192,1792]{1,0:T(8,128)(2,1)}), bf16[768,1792]{1,0:T(8,128)(2,1)}) %all-gather.10.cloned.1.call-update) | async-done | bytes 2752528 | tf_op jit(solution)/shard_map/all_gather | solution.py:64
  217.0 9.2 %convolution_convert_fusion.2 = bf16[4,1024,1792]{2,1,0:T(8,128)(2,1)} fusion(bf16[4,192,1792]{2,1,0:T(8,128)(2,1)} %bitcast.39, bf16[192,4,1024]{2,0,1:T(8,128)(2,1)S(1)} %all-to-all-done), kind=kOutput, calls=%fused_computation.2 | convolution fusion | flops 2825912320 | bytes 19005440 | tf_op jit(solution)/shard_map/jrd,jrf->jdf/dot_general | solution.py:19
  226.2 10.7 %reduce_sum.36 = bf16[1024,1792]{1,0:T(8,128)(2,1)} reduce(bf16[4,1024,1792]{2,1,0:T(8,128)(2,1)} %convolution_convert_fusion.2, bf16[]{:T(256)} %constant.15.clone.1), dimensions={0}, to_apply=%region_3.4 | reduce | flops 5505024 | bytes 18350082 | tf_op jit(solution)/shard_map/reduce_sum | solution.py:23
  237.0 16.9 %reduce-scatter.3.cloned.1.call-done = bf16[24,4096]{1,0:T(8,128)(2,1)} async-done(((bf16[192,4096]{1,0:T(8,128)(2,1)}), bf16[24,4096]{1,0:T(8,128)(2,1)}) %reduce-scatter.3.cloned.1.call-update) | async-done | bytes 196624 | tf_op jit(solution)/shard_map/reduce_scatter | solution.py:38
  253.9 35.5 %reduce-scatter.5.cloned.1.call-done = bf16[24,4096]{1,0:T(8,128)(2,1)} async-done(((bf16[192,4096]{1,0:T(8,128)(2,1)}), bf16[24,4096]{1,0:T(8,128)(2,1)}) %reduce-scatter.5.cloned.1.call-update) | async-done | bytes 196624 | tf_op jit(solution)/shard_map/reduce_scatter | solution.py:48
  289.3 0.0 copy-done.1
  (8 shorter events, 0.0 us)
Async XLA Ops:
  7.2 1.0 copy-start
  7.2 31.0 %all-gather.6.cloned.1.call-start = ((), (), s32[]{:S(2)}) async-start(), calls=%async_computation.4 | async-start | bytes 1769472 | tf_op jit(solution)/shard_map/all_gather | solution.py:33
  9.1 55.2 %all-gather.8.cloned.1.call-start = ((), (), s32[]{:S(2)}) async-start(), calls=%async_computation.6 | async-start | bytes 1769472 | tf_op jit(solution)/shard_map/all_gather | solution.py:44
  9.8 130.4 %all-gather.14.cloned.1.call-start = ((), (), s32[]{:S(2)}) async-start(), calls=%async_computation.10 | async-start | bytes 3440640 | tf_op jit(solution)/shard_map/all_gather | solution.py:63
  38.2 9.3 %copy-start.2 = (bf16[192,4096]{1,0:T(8,128)(2,1)S(1)}, bf16[192,4096]{1,0:T(8,128)(2,1)}, u32[]{:S(2)}) copy-start(bf16[192,4096]{1,0:T(8,128)(2,1)} %all-gather.6.cloned.1.call-done) | copy-start | bytes 4718596
  38.2 10.6 %copy-start.5 = (bf16[4096,1792]{1,0:T(8,128)(2,1)S(1)}, bf16[4096,1792]{1,0:T(8,128)(2,1)}, u32[]{:S(2)}) copy-start(bf16[4096,1792]{1,0:T(8,128)(2,1)} %param.8) | copy-start | bytes 44040196
  76.8 97.8 %all-gather.12.cloned.1.call-start = ((), (), s32[]{:S(2)}) async-start(), calls=%async_computation.9 | async-start | bytes 3440640 | tf_op jit(solution)/shard_map/all_gather | solution.py:65
  77.4 139.6 %all-gather.10.cloned.1.call-start = ((), (), s32[]{:S(2)}) async-start(), calls=%async_computation.8 | async-start | bytes 3440640 | tf_op jit(solution)/shard_map/all_gather | solution.py:64
  78.0 10.0 %copy-start.3 = (bf16[192,4096]{1,0:T(8,128)(2,1)S(1)}, bf16[192,4096]{1,0:T(8,128)(2,1)}, u32[]{:S(2)}) copy-start(bf16[192,4096]{1,0:T(8,128)(2,1)} %all-gather.8.cloned.1.call-done) | copy-start | bytes 4718596
  78.0 175.8 %reduce-scatter.3.cloned.1.call-start = ((), (), s32[]{:S(2)}) async-start(), calls=%async_computation.5 | async-start | bytes 1769472 | tf_op jit(solution)/shard_map/reduce_scatter | solution.py:38
  89.3 34.9 %all-to-all-start.1 = ((bf16[192,4,1024]{2,0,1:T(8,128)(2,1)}), bf16[192,4,1024]{2,0,1:T(8,128)(2,1)S(1)}, u32[]{:S(2)}, u32[]{:S(2)}) async-start(bf16[192,4,1024]{2,0,1:T(8,128)(2,1)} %bitcast.35), calls=%async_computation.3 | async-start | bytes 3145728 | tf_op jit(solution)/shard_map/all_to_all | solution.py:60
  93.1 1.3 copy-start.4
  124.3 25.5 %all-to-all-start = ((bf16[192,4,1024]{2,0,1:T(8,128)(2,1)}), bf16[192,4,1024]{2,0,1:T(8,128)(2,1)S(1)}, u32[]{:S(2)}, u32[]{:S(2)}) async-start(bf16[192,4,1024]{2,0,1:T(8,128)(2,1)} %bitcast.37), calls=%async_computation.2 | async-start | bytes 3145728 | tf_op jit(solution)/shard_map/all_to_all | solution.py:59
  127.8 161.5 %reduce-scatter.5.cloned.1.call-start = ((), (), s32[]{:S(2)}) async-start(), calls=%async_computation.7 | async-start | bytes 1769472 | tf_op jit(solution)/shard_map/reduce_scatter | solution.py:48
  226.2 63.1 %copy-start.1 = (bf16[32,4096]{1,0:T(8,128)(2,1)S(1)}, bf16[32,4096]{1,0:T(8,128)(2,1)}, u32[]{:S(2)}) copy-start(bf16[32,4096]{1,0:T(8,128)(2,1)} %param.6) | copy-start | bytes 786436
Sparse Core Ops, SparseCore 0:
  10.2 27.9 all-gather.5
  39.9 24.3 all-gather.7
  77.0 50.7 all-gather.13
  129.4 45.1 all-gather.11
  176.4 40.5 all-gather.9
  219.7 34.0 reduce-scatter.2
  256.7 32.5 reduce-scatter.4
where the time goes:
time: 297 us; the launch traced here: 296 us
  waiting for transfers between devices  148 us (50%)
  matrix products  88.8 us (30%)
  other arithmetic  33.7 us (11%)
  between operations  14.2 us (5%)
  starting transfers between devices  7.58 us (3%)
  local copies, waits for them, and re-layouts  3.98 us (1%)
    dot_general x3, matrix products, contract_cols(): lax.dot_general(left_matrix, right_matrix, (((1,), (1,)), ((), ())), pref...  36.6 us
    reduce_scatter x1, waiting for transfers between devices, on_device(): lax.psum_scatter((contract_cols(gate_back, gate_weight) + contract_cols(u...  35.5 us
    reduce_sum x3, other arithmetic, group_sum(): return jnp.sum(partials.astype(jnp.float32), axis=0)  32.8 us
    all_gather x1, waiting for transfers between devices, on_device(): token_rows = lax.all_gather(picked, 'dp', axis=0, tiled=True)  28.3 us
    dot_general x3, matrix products, group_sum(): jnp.einsum(form, left_blocks, right_blocks, preferred_element_type=jnp.fl...  28 us
    all_gather x1, waiting for transfers between devices, on_device(): lax.all_gather(up_back, 'seq', axis=0, tiled=True)  24.9 us
    all_to_all x1, waiting for transfers between devices, on_device(): lax.all_to_all(cotangent_rows, 'seq', split_axis=1, concat_axis=0, tiled=...  18.2 us
    reduce_scatter x1, waiting for transfers between devices, on_device(): lax.psum_scatter(jnp.dot(hidden, down_weight, preferred_element_type=jnp....  16.9 us
  transfers between devices with their start and end apart: 9, of which 7 were waited for; matrix products, arithmetic and copies ran while one was open for 37% of the time, Pallas kernels for 0%

commit v1 on v0

--- a/solution.py
+++ b/solution.py
@@ -2,6 +2,12 @@
 import jax.numpy as jnp
 from jax import lax
 from jax.sharding import PartitionSpec as P
+
+
+def exchange_blocks(block, axis, split, join):
+    parts = jnp.split(block, lax.axis_size(axis), axis=split)
+    received = lax.all_to_all(jnp.stack(parts), axis, 0, 0)
+    return jnp.concatenate(received, axis=join)
 
 
 def silu_parts(gate_proj):
@@ -57,7 +63,7 @@
     row_total = token_rows.shape[0]
     split_tokens, split_cotangent = (
         lax.all_to_all(token_rows, "seq", split_axis=1, concat_axis=0, tiled=True),
-        lax.all_to_all(cotangent_rows, "seq", split_axis=1, concat_axis=0, tiled=True),
+        exchange_blocks(cotangent_rows, "seq", 1, 0),
     )
     all_hidden, all_gate_back, all_up_back = (
         lax.all_gather(hidden, "seq", axis=0, tiled=True),

time: 297 us -> 297 us (level)
    all_gather x1, waiting for transfers between devices: 24.9 us -> 19.8 us  [on_device(): lax.all_gather(up_back, 'seq', axis=0, tiled=True)]
  transfers between devices with their start and end apart: 9 -> 9, of which waited for: 7 -> 8; matrix products, arithmetic and copies ran while one was open for 37% -> 37% of each run, Pallas kernels for 0% -> 0%
where the time goes in v1:
time: 297 us
  waiting for transfers between devices  147 us (49%)
  matrix products  89 us (30%)
  other arithmetic  35 us (12%)
  between operations  14.2 us (5%)
  starting transfers between devices  7.58 us (3%)
  local copies, waits for them, and re-layouts  4.2 us (1%)
    dot_general x3, matrix products, contract_cols(): lax.dot_general(left_matrix, right_matrix, (((1,), (1,)), ((), ())), pref...  37.5 us
    reduce_scatter x1, waiting for transfers between devices, on_device(): lax.psum_scatter((contract_cols(gate_back, gate_weight) + contract_cols(u...  35.5 us
    reduce_sum x3, other arithmetic, group_sum(): return jnp.sum(partials.astype(jnp.float32), axis=0)  32.8 us
    all_gather x1, waiting for transfers between devices, on_device(): token_rows = lax.all_gather(picked, 'dp', axis=0, tiled=True)  28.3 us
    dot_general x3, matrix products, group_sum(): jnp.einsum(form, left_blocks, right_blocks, preferred_element_type=jnp.fl...  27.6 us
    all_gather x1, waiting for transfers between devices, on_device(): lax.all_gather(up_back, 'seq', axis=0, tiled=True)  19.8 us
    all_to_all x1, waiting for transfers between devices, exchange_blocks(): received = lax.all_to_all(jnp.stack(parts), axis, 0, 0)  19.1 us
    reduce_scatter x1, waiting for transfers between devices, on_device(): lax.psum_scatter(jnp.dot(hidden, down_weight, preferred_element_type=jnp....  17 us
  transfers between devices with their start and end apart: 9, of which 8 were waited for; matrix products, arithmetic and copies ran while one was open for 37% of the time, Pallas kernels for 0%

profile of v1, /device:TPU:0, one launch (start us, length us, event | category | flops | bytes accessed | tf_op | source)
XLA Modules:
  0.0 296.6 jit_solution(4974576974688191667)
XLA Ops:
  7.2 0.0 copy-start
  7.2 0.0 all-gather.6.cloned.1.call-start
  7.2 0.7 fusion.8
  7.9 0.1 copy.13
  8.0 0.1 reduce-window.8
  8.1 0.1 add_reduce_fusion
  8.2 0.9 convolution_convert_fusion.4
  9.1 0.0 all-gather.6.cloned.1.call-update
  9.1 0.0 all-gather.8.cloned.1.call-start
  9.1 0.7 all-gather.8.cloned.1.call-update
  9.8 0.0 all-gather.14.cloned.1.call-start
  9.9 28.3 %all-gather.6.cloned.1.call-done = bf16[192,4096]{1,0:T(8,128)(2,1)} async-done(((bf16[24,4096]{1,0:T(8,128)(2,1)}), bf16[192,4096]{1,0:T(8,128)(2,1)}) %all-gather.6.cloned.1.call-update) | async-done | bytes 1572880 | tf_op jit(solution)/shard_map/all_gather | solution.py:39
  38.2 9.3 %fusion.11 = f32[192,1792]{1,0:T(8,128)S(1)} fusion(bf16[192,4096]{1,0:T(8,128)(2,1)} %all-gather.6.cloned.1.call-done, bf16[4096,1792]{1,0:T(8,128)(2,1)} %param.9), kind=kOutput, calls=%fused_computation.29 | convolution fusion | flops 2818572288 | bytes 17629184 | tf_op jit(solution)/shard_map/dot_general | solution.py:41
  47.5 1.3 copy-done.6
  48.8 4.2 %fusion.10 = f32[192,1792]{1,0:T(8,128)} fusion(bf16[192,4096]{1,0:T(8,128)(2,1)S(1)} %copy-done.2, bf16[4096,1792]{1,0:T(8,128)(2,1)S(1)} %copy-done.6), kind=kOutput, calls=%fused_computation.28 | convolution fusion | flops 2818572288 | bytes 17629184 | tf_op jit(solution)/shard_map/dot_general | solution.py:40
  53.0 11.3 %all-gather.8.cloned.1.call-done = bf16[192,4096]{1,0:T(8,128)(2,1)} async-done(((bf16[24,4096]{1,0:T(8,128)(2,1)}), bf16[192,4096]{1,0:T(8,128)(2,1)}) %all-gather.8.cloned.1.call-update) | async-done | bytes 1572880 | tf_op jit(solution)/shard_map/all_gather | solution.py:50
  64.3 12.5 %multiply_convert_fusion = (bf16[192,1792]{1,0:T(8,128)(2,1)}, bf16[192,1792]{1,0:T(8,128)(2,1)}, bf16[192,1792]{1,0:T(8,128)(2,1)}) fusion(f32[192,1792]{1,0:T(8,128)} %fusion.10, f32[192,1792]{1,0:T(8,128)S(1)} %fusion.11, bf16[192,4096]{1,0:T(8,128)(2,1)} %all-gather.8.cloned.1.call-done, bf16[1792,4096]{1,0:T(8,128)(2,1)} %param.10), kind=kOutput, calls=%fused_computation.11 | convolution fusion | flops 2823733248 | bytes 21069824 | tf_op jit(solution)/shard_map/dot_general | solution.py:19
  76.8 0.0 all-gather.14.cloned.1.call-update
  76.8 0.0 all-gather.12.cloned.1.call-start
  76.9 0.5 all-gather.12.cloned.1.call-update
  77.4 0.0 all-gather.10.cloned.1.call-start
  77.5 0.5 all-gather.10.cloned.1.call-update
  78.0 0.0 reduce-scatter.3.cloned.1.call-start
  78.1 9.5 %convolution_convert_fusion.3 = bf16[192,4096]{1,0:T(8,128)(2,1)} fusion(bf16[192,1792]{1,0:T(8,128)(2,1)S(1)} %copy-done.5, bf16[1792,4096]{1,0:T(8,128)(2,1)} %param.10), kind=kOutput, calls=%fused_computation.5 | convolution fusion | flops 2819358720 | bytes 16941056 | tf_op jit(solution)/shard_map/dot_general | solution.py:45
  87.6 0.0 reduce-scatter.3.cloned.1.call-update
  87.6 1.4 copy-done.3
  89.0 0.1 slice_bitcast_fusion.3
  89.1 1.3 pad_maximum_fusion
  90.5 3.7 %all-to-all-start.1 = ((bf16[4,192,1024]{2,1,0:T(8,128)(2,1)}), bf16[4,192,1024]{2,1,0:T(8,128)(2,1)S(1)}, u32[]{:S(2)}, u32[]{:S(2)}) async-start(bf16[4,192,1024]{2,1,0:T(8,128)(2,1)} %pad_maximum_fusion), calls=%async_computation.3 | async-start | bytes 3145728 | tf_op jit(solution)/shard_map/all_to_all | solution.py:9
  94.2 1.3 copy.17
  95.5 12.2 %fusion.12 = f32[192,4096]{1,0:T(8,128)} fusion(bf16[192,1792]{1,0:T(8,128)(2,1)S(1)} %copy-done.4, bf16[4096,1792]{1,0:T(8,128)(2,1)} %param.8), kind=kOutput, calls=%fused_computation.30 | convolution fusion | flops 2818572288 | bytes 18513920 | tf_op jit(solution)/shard_map/dot_general | solution.py:19
  107.7 19.1 %all-to-all-done.1 = bf16[4,192,1024]{2,1,0:T(8,128)(2,1)S(1)} async-done(((bf16[4,192,1024]{2,1,0:T(8,128)(2,1)}), bf16[4,192,1024]{2,1,0:T(8,128)(2,1)S(1)}, u32[]{:S(2)}, u32[]{:S(2)}) %all-to-all-start.1) | async-done | bytes 1572896 | tf_op jit(solution)/shard_map/all_to_all | solution.py:9
  126.9 3.6 %all-to-all-start = ((bf16[192,4,1024]{2,0,1:T(8,128)(2,1)}), bf16[192,4,1024]{2,0,1:T(8,128)(2,1)S(1)}, u32[]{:S(2)}, u32[]{:S(2)}) async-start(bf16[192,4,1024]{2,0,1:T(8,128)(2,1)} %bitcast.39), calls=%async_computation.2 | async-start | bytes 3145728 | tf_op jit(solution)/shard_map/all_to_all | solution.py:65
  130.4 0.0 reduce-scatter.5.cloned.1.call-start
  130.5 12.8 %fusion = bf16[192,4096]{1,0:T(8,128)(2,1)} fusion(f32[192,4096]{1,0:T(8,128)} %fusion.12, bf16[192,1792]{1,0:T(8,128)(2,1)} %get-tuple-element.5, bf16[4096,1792]{1,0:T(8,128)(2,1)} %param.9), kind=kOutput, calls=%fused_computation.4 | convolution fusion | flops 2820145152 | bytes 20086784 | tf_op jit(solution)/shard_map/dot_general | solution.py:19
  143.3 0.0 reduce-scatter.5.cloned.1.call-update
  143.3 0.0 all-gather.14.cloned.1.call-done
  143.3 9.2 %convolution_convert_fusion = bf16[4,1792,1024]{2,1,0:T(8,128)(2,1)} fusion(bf16[4,192,1792]{2,1,0:T(8,128)(2,1)} %bitcast.42, bf16[4,192,1024]{2,1,0:T(8,128)(2,1)S(1)} %all-to-all-done.1), kind=kOutput, calls=%fused_computation | convolution fusion | flops 2825912320 | bytes 19005440 | tf_op jit(solution)/shard_map/jrf,jrd->jfd/dot_general | solution.py:25
  152.6 2.7 all-to-all-done
  155.3 19.8 %all-gather.12.cloned.1.call-done = bf16[768,1792]{1,0:T(8,128)(2,1)} async-done(((bf16[192,1792]{1,0:T(8,128)(2,1)}), bf16[768,1792]{1,0:T(8,128)(2,1)}) %all-gather.12.cloned.1.call-update) | async-done | bytes 2752528 | tf_op jit(solution)/shard_map/all_gather | solution.py:71
  175.1 9.2 %convolution_convert_fusion.1 = bf16[4,1024,1792]{2,1,0:T(8,128)(2,1)} fusion(bf16[4,192,1792]{2,1,0:T(8,128)(2,1)} %bitcast.40, bf16[192,4,1024]{2,0,1:T(8,128)(2,1)S(1)} %all-to-all-done), kind=kOutput, calls=%fused_computation.1 | convolution fusion | flops 2825912320 | bytes 19005440 | tf_op jit(solution)/shard_map/jrd,jrf->jdf/dot_general | solution.py:25
  184.3 11.1 %reduce_sum.38 = bf16[1792,1024]{1,0:T(8,128)(2,1)} reduce(bf16[4,1792,1024]{2,1,0:T(8,128)(2,1)} %convolution_convert_fusion, bf16[]{:T(256)} %constant.15.clone.1), dimensions={0}, to_apply=%region_5.6 | reduce | flops 5505024 | bytes 18350082 | tf_op jit(solution)/shard_map/reduce_sum | solution.py:29
  195.5 10.9 %reduce_sum.37 = bf16[1024,1792]{1,0:T(8,128)(2,1)} reduce(bf16[4,1024,1792]{2,1,0:T(8,128)(2,1)} %convolution_convert_fusion.1, bf16[]{:T(256)} %constant.15.clone.1), dimensions={0}, to_apply=%region_4.5 | reduce | flops 5505024 | bytes 18350082 | tf_op jit(solution)/shard_map/reduce_sum | solution.py:29
  206.4 11.0 %all-gather.10.cloned.1.call-done = bf16[768,1792]{1,0:T(8,128)(2,1)} async-done(((bf16[192,1792]{1,0:T(8,128)(2,1)}), bf16[768,1792]{1,0:T(8,128)(2,1)}) %all-gather.10.cloned.1.call-update) | async-done | bytes 2752528 | tf_op jit(solution)/shard_map/all_gather | solution.py:70
  217.4 9.2 %convolution_convert_fusion.2 = bf16[4,1024,1792]{2,1,0:T(8,128)(2,1)} fusion(bf16[4,192,1792]{2,1,0:T(8,128)(2,1)} %bitcast.41, bf16[192,4,1024]{2,0,1:T(8,128)(2,1)S(1)} %all-to-all-done), kind=kOutput, calls=%fused_computation.2 | convolution fusion | flops 2825912320 | bytes 19005440 | tf_op jit(solution)/shard_map/jrd,jrf->jdf/dot_general | solution.py:25
  226.6 10.7 %reduce_sum.36 = bf16[1024,1792]{1,0:T(8,128)(2,1)} reduce(bf16[4,1024,1792]{2,1,0:T(8,128)(2,1)} %convolution_convert_fusion.2, bf16[]{:T(256)} %constant.15.clone.1), dimensions={0}, to_apply=%region_3.4 | reduce | flops 5505024 | bytes 18350082 | tf_op jit(solution)/shard_map/reduce_sum | solution.py:29
  237.3 17.0 %reduce-scatter.3.cloned.1.call-done = bf16[24,4096]{1,0:T(8,128)(2,1)} async-done(((bf16[192,4096]{1,0:T(8,128)(2,1)}), bf16[24,4096]{1,0:T(8,128)(2,1)}) %reduce-scatter.3.cloned.1.call-update) | async-done | bytes 196624 | tf_op jit(solution)/shard_map/reduce_scatter | solution.py:44
  254.3 35.5 %reduce-scatter.5.cloned.1.call-done = bf16[24,4096]{1,0:T(8,128)(2,1)} async-done(((bf16[192,4096]{1,0:T(8,128)(2,1)}), bf16[24,4096]{1,0:T(8,128)(2,1)}) %reduce-scatter.5.cloned.1.call-update) | async-done | bytes 196624 | tf_op jit(solution)/shard_map/reduce_scatter | solution.py:54
  (11 shorter events, 0.0 us)
Async XLA Ops:
  7.2 1.0 copy-start
  7.2 31.0 %all-gather.6.cloned.1.call-start = ((), (), s32[]{:S(2)}) async-start(), calls=%async_computation.4 | async-start | bytes 1769472 | tf_op jit(solution)/shard_map/all_gather | solution.py:39
  9.1 55.2 %all-gather.8.cloned.1.call-start = ((), (), s32[]{:S(2)}) async-start(), calls=%async_computation.6 | async-start | bytes 1769472 | tf_op jit(solution)/shard_map/all_gather | solution.py:50
  9.8 133.5 %all-gather.14.cloned.1.call-start = ((), (), s32[]{:S(2)}) async-start(), calls=%async_computation.10 | async-start | bytes 3440640 | tf_op jit(solution)/shard_map/all_gather | solution.py:69
  38.2 9.3 %copy-start.2 = (bf16[192,4096]{1,0:T(8,128)(2,1)S(1)}, bf16[192,4096]{1,0:T(8,128)(2,1)}, u32[]{:S(2)}) copy-start(bf16[192,4096]{1,0:T(8,128)(2,1)} %all-gather.6.cloned.1.call-done) | copy-start | bytes 4718596
  38.2 10.6 %copy-start.6 = (bf16[4096,1792]{1,0:T(8,128)(2,1)S(1)}, bf16[4096,1792]{1,0:T(8,128)(2,1)}, u32[]{:S(2)}) copy-start(bf16[4096,1792]{1,0:T(8,128)(2,1)} %param.8) | copy-start | bytes 44040196
  76.8 1.2 copy-start.5
  76.8 98.2 %all-gather.12.cloned.1.call-start = ((), (), s32[]{:S(2)}) async-start(), calls=%async_computation.9 | async-start | bytes 3440640 | tf_op jit(solution)/shard_map/all_gather | solution.py:71
  77.4 140.0 %all-gather.10.cloned.1.call-start = ((), (), s32[]{:S(2)}) async-start(), calls=%async_computation.8 | async-start | bytes 3440640 | tf_op jit(solution)/shard_map/all_gather | solution.py:70
  78.0 176.2 %reduce-scatter.3.cloned.1.call-start = ((), (), s32[]{:S(2)}) async-start(), calls=%async_computation.5 | async-start | bytes 1769472 | tf_op jit(solution)/shard_map/reduce_scatter | solution.py:44
  87.6 1.4 copy-start.3
  90.5 36.4 %all-to-all-start.1 = ((bf16[4,192,1024]{2,1,0:T(8,128)(2,1)}), bf16[4,192,1024]{2,1,0:T(8,128)(2,1)S(1)}, u32[]{:S(2)}, u32[]{:S(2)}) async-start(bf16[4,192,1024]{2,1,0:T(8,128)(2,1)} %pad_maximum_fusion), calls=%async_computation.3 | async-start | bytes 3145728 | tf_op jit(solution)/shard_map/all_to_all | solution.py:9
  94.2 1.3 copy-start.4
  126.9 28.4 %all-to-all-start = ((bf16[192,4,1024]{2,0,1:T(8,128)(2,1)}), bf16[192,4,1024]{2,0,1:T(8,128)(2,1)S(1)}, u32[]{:S(2)}, u32[]{:S(2)}) async-start(bf16[192,4,1024]{2,0,1:T(8,128)(2,1)} %bitcast.39), calls=%async_computation.2 | async-start | bytes 3145728 | tf_op jit(solution)/shard_map/all_to_all | solution.py:65
  130.4 159.3 %reduce-scatter.5.cloned.1.call-start = ((), (), s32[]{:S(2)}) async-start(), calls=%async_computation.7 | async-start | bytes 1769472 | tf_op jit(solution)/shard_map/reduce_scatter | solution.py:54
  226.6 63.2 %copy-start.1 = (bf16[32,4096]{1,0:T(8,128)(2,1)S(1)}, bf16[32,4096]{1,0:T(8,128)(2,1)}, u32[]{:S(2)}) copy-start(bf16[32,4096]{1,0:T(8,128)(2,1)} %param.6) | copy-start | bytes 786436
Sparse Core Ops, SparseCore 0:
  10.2 27.9 all-gather.5
  39.9 24.3 all-gather.7
  77.0 51.9 all-gather.13
  130.6 44.4 all-gather.11
  176.8 40.5 all-gather.9
  220.1 34.0 reduce-scatter.2
  257.1 32.5 reduce-scatter.4
